TPU v7x, 256 devices: a whole 4x4x8 slice. The times are simulated.
256 devices in a mesh: row: 32 (over y, z), col: 8 (over x, core).
Axes of the slice: x: 4, y: 4, z: 8, core: 2. Of those that a mesh axis runs over, the one named last changes fastest.
Arguments:
- responses: bfloat16 [4096, 2, 3, 2048], P(('col', 'row')), may hold values from -6 to 6
- labels: int32 [2048], replicated, may hold values from 0 to 15
- conductivity: float32 [16], replicated, may hold values from 0.05 to 2
- permittivity: float32 [16], replicated, may hold values from 0.1 to 1.6
Outputs:
- noise_cov: float32 [2, 4096, 4096], P(None, 'row', 'col')
- energy_gram: float32 [2, 4096, 4096], P(None, 'row', 'col')
All inputs are finite; a program needn't handle non-finite values.
Results may differ from a plain program's by a relative error of at most 0.0021.
Values may be sent and summed in bfloat16 or wider, within the bound.
No kernel may reach another device: no remote copies, remote signals or barrier semaphores. Data moves between devices by JAX's collectives and lax.ppermute only.
A program may use at most 128 MiB of HBM per device.

v0:
```python
import jax
import jax.numpy as jnp
from jax import lax
from jax.sharding import PartitionSpec as P


def broadcast(block, axis, holder):
    block = jnp.where(lax.axis_index(axis) == holder, block, jnp.zeros_like(block))
    return lax.psum(block, axis)


def tile_products(row_fields, right_fields, vox_labels, conductivity, permittivity, scale_factor):
    classes = jnp.arange(conductivity.shape[0], dtype=jnp.int32)
    onehot = (vox_labels[None, :] == classes[:, None]).astype(jnp.float32)
    cond_voxel = jnp.sum(onehot * conductivity[:, None], axis=0) * scale_factor
    perm_voxel = jnp.sum(onehot * permittivity[:, None], axis=0) * scale_factor
    fields = row_fields.astype(jnp.float32)
    vox_here = row_fields.shape[3]
    row_total = row_fields.shape[0]

    def weighted(weight_vec):
        scaled = fields * weight_vec[None, None, None, :]
        crossed = jnp.concatenate([-scaled[:, 1:2], scaled[:, 0:1]], axis=1)
        return (scaled.astype(jnp.bfloat16), crossed.astype(jnp.bfloat16))

    sig_plain, sig_cross = weighted(cond_voxel)
    eps_plain, eps_cross = weighted(perm_voxel)
    left_stack = jnp.concatenate([sig_plain, sig_cross, eps_plain, eps_cross], axis=0)
    left_stack = left_stack.reshape(4 * row_total, 6 * vox_here)
    right_flat = right_fields.reshape(right_fields.shape[0], 6 * vox_here)
    products = lax.dot_general(
        left_stack, right_flat, (((1,), (1,)), ((), ())), preferred_element_type=jnp.float32
    )
    return products.reshape(4, row_total, right_fields.shape[0])


def body(responses, labels, conductivity, permittivity):
    nb_dev = responses.shape[0]
    vox_total = labels.shape[0]
    row_count = lax.axis_size("row")
    col_count = lax.axis_size("col")
    row_block = nb_dev * col_count
    row_index = lax.axis_index("row")
    scale_factor = 1.0 / jnp.sqrt(jnp.float32(6 * vox_total))
    columns = lax.all_gather(responses, "row", axis=0, tiled=True)
    row_ratio = row_count // col_count
    own_rows = lax.dynamic_slice_in_dim(columns, row_index % row_ratio * row_block, row_block, 0)
    row_fields = broadcast(own_rows, "col", row_index // row_ratio)
    products = tile_products(row_fields, columns, labels, conductivity, permittivity, scale_factor)
    noise_cov = products[0:2]
    energy_gram = products[2:4]
    return (noise_cov, energy_gram)


def solution(mesh):
    in_specs = (P(("col", "row"), None, None, None), P(), P(), P())
    out_specs = (P(None, "row", "col"), P(None, "row", "col"))
    return jax.shard_map(body, mesh=mesh, in_specs=in_specs, out_specs=out_specs, check_vma=False)
```

profile of v0, /device:TPU:8, one launch (start us, length us, event | category | flops | bytes accessed | tf_op | source)
XLA Modules:
  0.0 240.6 jit_solution(9226071765441624125)
XLA Ops:
  7.2 0.0 copy-start.4
  7.2 0.0 copy-start.3
  7.2 0.0 copy-start.2
  7.2 0.0 all-gather.2.cloned.1.call-start
  7.2 1.9 copy.7
  9.1 0.0 all-gather.2.cloned.1.call-update
  9.1 0.0 all-reduce.2.cloned.1.call-start
  9.2 123.3 %all-gather.2.cloned.1.call-done = bf16[512,2,3,2048]{3,0,2,1:T(8,128)(2,1)} async-done(((bf16[16,2,3,2048]{3,0,2,1:T(8,128)(2,1)}), bf16[512,2,3,2048]{3,0,2,1:T(8,128)(2,1)}) %all-gather.2.cloned.1.call-update) | async-done | bytes 12582928 | tf_op jit(solution)/shard_map/all_gather | solution.py:45
  132.5 4.5 %dynamic-slice_select_fusion = bf16[128,2,3,2048]{3,0,2,1:T(8,128)(2,1)} fusion(bf16[512,2,3,2048]{3,0,2,1:T(8,128)(2,1)} %all-gather.2.cloned.1.call-done, s32[]{:T(128)S(6)} %select_n.25, pred[]{:T(512)S(6)} %eq.18), kind=kLoop, calls=%fused_computation.18 | loop fusion | flops 1572864 | bytes 6291461 | tf_op jit(solution)/shard_map/jit(_where)/select_n | solution.py:8
  137.0 0.0 all-reduce.2.cloned.1.call-update
  137.0 0.0 copy-done.4
  137.0 0.0 copy-done.3
  137.1 0.0 copy-done.2
  137.1 0.1 select_reduce_fusion.1
  137.2 72.5 %all-reduce.2.cloned.1.call-done = bf16[128,2,3,2048]{3,0,2,1:T(8,128)(2,1)} async-done(((bf16[128,2,3,2048]{3,0,2,1:T(8,128)(2,1)}), bf16[128,2,3,2048]{3,0,2,1:T(8,128)(2,1)}) %all-reduce.2.cloned.1.call-update) | async-done | bytes 3145744 | tf_op jit(solution)/shard_map/psum | solution.py:9
  209.7 6.8 %convert_multiply_fusion.1 = (f32[128,2,3,2048]{3,0,2,1:T(8,128)S(1)}, bf16[128,2,3,2048]{3,0,2,1:T(8,128)(2,1)}, bf16[128,2,3,2048]{3,0,2,1:T(8,128)(2,1)}, f32[128,2,3,2048]{3,0,2,1:T(8,128)S(1)}) fusion(bf16[128,2,3,2048]{3,0,2,1:T(8,128)(2,1)} %all-reduce.2.cloned.1.call-done, f32[2048]{0:T(1024)S(1)} %get-tuple-element.13, f32[2048]{0:T(1024)S(1)} %get-tuple-element.12), kind=kLoop, calls=%fused_computation.13 | loop fusion | flops 7864320 | bytes 22036480 | tf_op jit(solution)/shard_map/mul | solution.py:22
  216.5 0.0 copy-start
  216.5 0.0 copy-start.1
  216.5 0.2 fusion.13
  216.7 0.2 fusion.12
  217.0 1.4 copy-done
  218.4 0.2 slice.35
  218.5 0.8 copy-done.1
  219.3 0.2 slice.37
  219.5 13.2 %fusion.14 = f32[512,512]{1,0:T(8,128)S(1)} fusion(bf16[512,2,3,2048]{3,0,2,1:T(8,128)(2,1)} %all-gather.2.cloned.1.call-done, bf16[128,1,3,2048]{3,0,2,1:T(8,128)(2,1)S(1)} %slice.37, bf16[128,1,3,2048]{3,0,2,1:T(8,128)(2,1)S(1)} %fusion.12, bf16[128,2,3,2048]{3,0,2,1:T(8,128)(2,1)S(1)} %copy-done.1, bf16[128,1,3,2048]{3,0,2,1:T(8,128)(2,1)S(1)} %slice.35, ...), kind=kOutput, calls=%fused_computation.19 | convolution fusion | flops 6517948416 | bytes 26214400 | tf_op jit(solution)/shard_map/dot_general | solution.py:31
  232.7 1.0 fusion.20
  (1 shorter events, 0.0 us)
Async XLA Ops:
  7.2 129.9 %copy-start.4 = (f32[16]{0:T(128)S(1)}, f32[16]{0:T(128)}, u32[]{:S(2)}) copy-start(f32[16]{0:T(128)} %param.7) | copy-start | bytes 196
  7.2 129.9 %copy-start.3 = (f32[16]{0:T(128)S(1)}, f32[16]{0:T(128)}, u32[]{:S(2)}) copy-start(f32[16]{0:T(128)} %param.6) | copy-start | bytes 196
  7.2 129.9 %copy-start.2 = (s32[2048]{0:T(1024)S(1)}, s32[2048]{0:T(1024)}, u32[]{:S(2)}) copy-start(s32[2048]{0:T(1024)} %param.5) | copy-start | bytes 24580
  7.2 125.3 %all-gather.2.cloned.1.call-start = ((), (), s32[]{:S(2)}) async-start(), calls=%async_computation | async-start | bytes 12976128 | tf_op jit(solution)/shard_map/all_gather | solution.py:45
  9.1 200.5 %all-reduce.2.cloned.1.call-start = ((), (), s32[]{:S(2)}) async-start(), calls=%async_computation.1 | async-start | bytes 6291456 | tf_op jit(solution)/shard_map/psum | solution.py:9
  216.5 1.9 copy-start
  216.5 2.8 %copy-start.1 = (bf16[128,2,3,2048]{3,0,2,1:T(8,128)(2,1)S(1)}, bf16[128,2,3,2048]{3,0,2,1:T(8,128)(2,1)}, u32[]{:S(2)}) copy-start(bf16[128,2,3,2048]{3,0,2,1:T(8,128)(2,1)} %get-tuple-element.8) | copy-start | bytes 9437188
Sparse Core Ops, SparseCore 0:
  11.2 121.3 all-gather.1
  137.2 72.4 all-reduce.1
where the time goes:
time: 241 us
  waiting for transfers between devices  196 us (81%)
  between operations  14.2 us (6%)
  matrix products  13.2 us (5%)
  other arithmetic  11.9 us (5%)
  local copies, waits for them, and re-layouts  5.42 us (2%)
    all_gather x1, waiting for transfers between devices, body(): columns = lax.all_gather(responses, 'row', axis=0, tiled=True)  123 us
    psum x1, waiting for transfers between devices, broadcast(): return lax.psum(block, axis)  72.5 us
    dot_general x1, matrix products, tile_products(): lax.dot_general(left_stack, right_flat, (((1,), (1,)), ((), ())), preferr...  13.2 us
    mul x1, other arithmetic, weighted(): scaled = fields * weight_vec[None, None, None, :]  6.83 us
  transfers between devices with their start and end apart: 2, of which 2 were waited for; matrix products, arithmetic and copies ran while one was open for 0% of the time, Pallas kernels for 0%

commit v1 on v0

--- a/solution.py
+++ b/solution.py
@@ -2,6 +2,12 @@
 import jax.numpy as jnp
 from jax import lax
 from jax.sharding import PartitionSpec as P
+
+
+def gather_by_exchange(x, axis, dim):
+    size = lax.axis_size(axis)
+    repeats = [size if d == dim else 1 for d in range(x.ndim)]
+    return lax.all_to_all(jnp.tile(x, repeats), axis, split_axis=dim, concat_axis=dim, tiled=True)
 
 
 def broadcast(block, axis, holder):
@@ -42,7 +48,7 @@
     row_block = nb_dev * col_count
     row_index = lax.axis_index("row")
     scale_factor = 1.0 / jnp.sqrt(jnp.float32(6 * vox_total))
-    columns = lax.all_gather(responses, "row", axis=0, tiled=True)
+    columns = gather_by_exchange(responses, "row", 0)
     row_ratio = row_count // col_count
     own_rows = lax.dynamic_slice_in_dim(columns, row_index % row_ratio * row_block, row_block, 0)
     row_fields = broadcast(own_rows, "col", row_index // row_ratio)

time: 241 us -> 453 us (1.88)
  waiting for transfers between devices: 196 us -> 377 us
  local copies, waits for them, and re-layouts: 5.42 us -> 26.7 us
  starting transfers between devices: 0.08 us -> 11.8 us
    all_to_all x0 -> x1, waiting for transfers between devices: none -> 295 us  [gather_by_exchange(): lax.all_to_all(jnp.tile(x, repeats), axis, split_axis=dim, concat_axis=di...]
    all_gather x1 -> x0, waiting for transfers between devices: 123 us -> none  [body(): columns = lax.all_gather(responses, 'row', axis=0, tiled=True)]
    another operation x0 -> x1, local copies, waits for them, and re-layouts: none -> 13.7 us  [gather_by_exchange(): jnp.tile(x, repeats)]
    all_to_all x0 -> x1, starting transfers between devices: none -> 11.8 us  [gather_by_exchange(): lax.all_to_all(jnp.tile(x, repeats), axis, split_axis=dim, concat_axis=di...]
    psum x1, waiting for transfers between devices: 72.5 us -> 82.1 us  [broadcast(): return lax.psum(block, axis)]
    all_to_all x0 -> x1, local copies, waits for them, and re-layouts: none -> 9.4 us  [gather_by_exchange(): lax.all_to_all(jnp.tile(x, repeats), axis, split_axis=dim, concat_axis=di...]
where the time goes in v1:
time: 453 us
  waiting for transfers between devices  377 us (83%)
  local copies, waits for them, and re-layouts  26.7 us (6%)
  between operations  14.2 us (3%)
  matrix products  13.3 us (3%)
  starting transfers between devices  11.8 us (3%)
  other arithmetic  9.98 us (2%)
    all_to_all x1, waiting for transfers between devices, gather_by_exchange(): lax.all_to_all(jnp.tile(x, repeats), axis, split_axis=dim, concat_axis=di...  295 us
    psum x1, waiting for transfers between devices, broadcast(): return lax.psum(block, axis)  82.1 us
    another operation x1, local copies, waits for them, and re-layouts, gather_by_exchange(): jnp.tile(x, repeats)  13.7 us
    dot_general x1, matrix products, tile_products(): lax.dot_general(left_stack, right_flat, (((1,), (1,)), ((), ())), preferr...  13.3 us
    all_to_all x1, starting transfers between devices, gather_by_exchange(): lax.all_to_all(jnp.tile(x, repeats), axis, split_axis=dim, concat_axis=di...  11.8 us
    all_to_all x1, local copies, waits for them, and re-layouts, gather_by_exchange(): lax.all_to_all(jnp.tile(x, repeats), axis, split_axis=dim, concat_axis=di...  9.4 us
  transfers between devices with their start and end apart: 2, of which 2 were waited for; matrix products, arithmetic and copies ran while one was open for 0% of the time, Pallas kernels for 0%

profile of v1, /device:TPU:8, one launch (start us, length us, event | category | flops | bytes accessed | tf_op | source)
XLA Modules:
  0.0 452.8 jit_solution(5138628465667718333)
XLA Ops:
  7.2 13.7 %tile.4 = bf16[32,16,2,3,2048]{4,2,3,1,0:T(2,128)(2,1)} broadcast(bf16[16,2,3,2048]{3,1,2,0:T(2,128)(2,1)} %param.4), dimensions={1,2,3,4} | broadcast | bytes 12976128 | tf_op jit(solution)/shard_map/tile | solution.py:10
  20.9 11.8 %all-to-all-start = ((bf16[512,2,3,2048]{3,1,2,0:T(2,128)(2,1)}), bf16[512,2,3,2048]{3,1,2,0:T(2,128)(2,1)}, u32[]{:S(2)}, u32[]{:S(2)}) async-start(bf16[512,2,3,2048]{3,1,2,0:T(2,128)(2,1)} %bitcast.7), calls=%async_computation | async-start | bytes 25165824 | tf_op jit(solution)/shard_map/all_to_all | solution.py:10
  32.6 0.0 all-reduce.2.cloned.1.call-start
  32.7 294.8 %all-to-all-done = bf16[512,2,3,2048]{3,1,2,0:T(2,128)(2,1)} async-done(((bf16[512,2,3,2048]{3,1,2,0:T(2,128)(2,1)}), bf16[512,2,3,2048]{3,1,2,0:T(2,128)(2,1)}, u32[]{:S(2)}, u32[]{:S(2)}) %all-to-all-start) | async-done | bytes 12582944 | tf_op jit(solution)/shard_map/all_to_all | solution.py:10
  327.5 9.4 %copy.12 = bf16[512,2,3,2048]{3,0,2,1:T(8,128)(2,1)S(1)} copy(bf16[512,2,3,2048]{3,1,2,0:T(2,128)(2,1)} %all-to-all-done) | data formatting | bytes 25165824 | tf_op jit(solution)/shard_map/all_to_all | solution.py:10
  336.9 0.0 copy-start.2
  336.9 0.0 copy-start.3
  336.9 0.0 copy-start.4
  336.9 2.6 dynamic-slice_select_fusion
  339.5 0.0 all-reduce.2.cloned.1.call-update
  339.5 0.0 copy-done.2
  339.5 0.0 copy-done.3
  339.5 0.0 copy-done.4
  339.5 0.1 select_reduce_fusion.1
  339.7 82.1 %all-reduce.2.cloned.1.call-done = bf16[128,2,3,2048]{3,0,2,1:T(8,128)(2,1)} async-done(((bf16[128,2,3,2048]{3,0,2,1:T(8,128)(2,1)}), bf16[128,2,3,2048]{3,0,2,1:T(8,128)(2,1)}) %all-reduce.2.cloned.1.call-update) | async-done | bytes 3145744 | tf_op jit(solution)/shard_map/psum | solution.py:15
  421.8 6.8 %convert_multiply_fusion.1 = (f32[128,2,3,2048]{3,0,2,1:T(8,128)S(1)}, bf16[128,2,3,2048]{3,0,2,1:T(8,128)(2,1)}, bf16[128,2,3,2048]{3,0,2,1:T(8,128)(2,1)}, f32[128,2,3,2048]{3,0,2,1:T(8,128)S(1)}) fusion(bf16[128,2,3,2048]{3,0,2,1:T(8,128)(2,1)} %all-reduce.2.cloned.1.call-done, f32[2048]{0:T(1024)S(1)} %get-tuple-element.13, f32[2048]{0:T(1024)S(1)} %get-tuple-element.12), kind=kLoop, calls=%fused_computation.13 | loop fusion | flops 7864320 | bytes 22036480 | tf_op jit(solution)/shard_map/mul | solution.py:28
  428.6 0.0 copy-start
  428.6 0.0 copy-start.1
  428.6 0.2 fusion.13
  428.9 0.2 fusion.12
  429.1 1.4 copy-done
  430.5 0.2 slice.35
  430.7 0.8 copy-done.1
  431.5 0.2 slice.37
  431.6 13.3 %fusion.14 = f32[512,512]{1,0:T(8,128)S(1)} fusion(bf16[128,1,3,2048]{3,0,2,1:T(8,128)(2,1)S(1)} %slice.37, bf16[128,1,3,2048]{3,0,2,1:T(8,128)(2,1)S(1)} %fusion.12, bf16[128,2,3,2048]{3,0,2,1:T(8,128)(2,1)S(1)} %copy-done.1, bf16[128,1,3,2048]{3,0,2,1:T(8,128)(2,1)S(1)} %slice.35, bf16[128,1,3,2048]{3,0,2,1:T(8,128)(2,1)S(1)} %fusion.13, ...), kind=kOutput, calls=%fused_computation.19 | convolution fusion | flops 6517948416 | bytes 26214400 | tf_op jit(solution)/shard_map/dot_general | solution.py:37
  445.0 1.0 fusion.21
  (1 shorter events, 0.0 us)
Async XLA Ops:
  20.9 306.6 %all-to-all-start = ((bf16[512,2,3,2048]{3,1,2,0:T(2,128)(2,1)}), bf16[512,2,3,2048]{3,1,2,0:T(2,128)(2,1)}, u32[]{:S(2)}, u32[]{:S(2)}) async-start(bf16[512,2,3,2048]{3,1,2,0:T(2,128)(2,1)} %bitcast.7), calls=%async_computation | async-start | bytes 25165824 | tf_op jit(solution)/shard_map/all_to_all | solution.py:10
  32.6 389.2 %all-reduce.2.cloned.1.call-start = ((), (), s32[]{:S(2)}) async-start(), calls=%async_computation.1 | async-start | bytes 6291456 | tf_op jit(solution)/shard_map/psum | solution.py:15
  336.9 2.6 copy-start.2
  336.9 2.6 copy-start.3
  336.9 2.6 copy-start.4
  428.6 1.9 copy-start
  428.6 2.8 copy-start.1
Sparse Core Ops, SparseCore 0:
  339.6 82.1 all-reduce.1
